TPU v7x, 32 devices: a whole 2x2x4 slice. The times are simulated.
32 devices in a mesh: pipe: 4 (over x, core), expert: 8 (over z, y).
Axes of the slice: x: 2, y: 2, z: 4, core: 2. Of those that a mesh axis runs over, the one named last changes fastest.
Arguments:
- tokens: bfloat16 [1024, 6144], P('expert'), may hold values from -6 to 6
- expert_ids: int32 [1024, 2], P('expert'), may hold values from 0 to 7, as said below
- gate_weight: bfloat16 [6144, 16384], P(None, 'expert'), may hold values from -0.078125 to 0.078125
- up_weight: bfloat16 [6144, 16384], P(None, 'expert'), may hold values from -0.078125 to 0.078125
- d_hidden: bfloat16 [256, 16384], P('pipe', 'expert'), may hold values from -6 to 6
Outputs:
- hidden: bfloat16 [256, 16384], P('pipe', 'expert')
- d_tokens: float32 [1024, 6144], P('expert', 'pipe')
Inputs may be any that keep to these rules, and one draw needn't show every extreme that they name: `expert_ids`: the two ids of a token differ. Among the 128 tokens of one block at least 8 and at most 32 name expert 0, and in every draw some block has exactly 32 such tokens.
All inputs are finite; a program needn't handle non-finite values.
Results may differ from a plain program's by a relative error of at most 0.0029.
Values may be sent and summed in bfloat16 or wider, within the bound.
A program may use at most 128 MiB of HBM per device.

v0:
```python
import functools

import jax
import jax.numpy as jnp
from jax import lax
from jax.experimental import pallas as pl
from jax.experimental.pallas import tpu as pltpu
from jax.sharding import PartitionSpec as P

CAP = 32
CORES = 2
UNIT = 16
STEPS = 6
Y_LAG, C_LAG = 3, 4
ADD_LAG, Y_SUM_LAG, Z_SUM_LAG = 1, 3, 6
MESH_ID = pl.DeviceIdType.MESH


def slot_select(expert_ids, first_slot, slot_count):
    is_named = jnp.any(expert_ids == 0, axis=1).astype(jnp.int32)
    slot_before = jnp.cumsum(is_named) - is_named
    positions = first_slot + jnp.arange(slot_count, dtype=jnp.int32)
    marked = (is_named[:, None] == 1) & (slot_before[:, None] == positions[None, :])
    return marked.astype(jnp.float32)


def plain_body(tokens, expert_ids, gate_weight, up_weight, d_hidden):
    hidden_units = gate_weight.shape[1]
    slot_span = CAP // lax.axis_size("pipe")
    own_select = slot_select(expert_ids, lax.axis_index("pipe") * slot_span, slot_span)
    routed = jnp.einsum(
        "tj,td->jd", own_select.astype(jnp.bfloat16), tokens, preferred_element_type=jnp.float32
    ).astype(jnp.bfloat16)
    piece = lax.all_gather(routed, "expert", axis=0, tiled=True)
    gate_part = jnp.dot(piece, gate_weight, preferred_element_type=jnp.float32)
    up_part = jnp.dot(piece, up_weight, preferred_element_type=jnp.float32)
    joined = jnp.concatenate([gate_part, up_part], axis=1)
    gate_value = joined[:, :hidden_units]
    up_value = joined[:, hidden_units:]
    sigmoid_gate = jax.nn.sigmoid(gate_value)
    activated = gate_value * sigmoid_gate
    hidden = (activated * up_value).astype(jnp.bfloat16)
    upstream = d_hidden.astype(jnp.float32)
    d_gate = (
        upstream * up_value * sigmoid_gate * (1.0 + gate_value * (1.0 - sigmoid_gate))
    ).astype(jnp.bfloat16)
    d_up = (upstream * activated).astype(jnp.bfloat16)
    result = jnp.einsum("nh,dh->nd", d_gate, gate_weight, preferred_element_type=jnp.float32)
    slot_grads = lax.psum_scatter(
        result + jnp.einsum("nh,dh->nd", d_up, up_weight, preferred_element_type=jnp.float32),
        "expert",
        scatter_dimension=0,
        tiled=True,
    )
    pieces = lax.all_to_all(slot_grads, "pipe", split_axis=1, concat_axis=0, tiled=True)
    full_select = slot_select(expert_ids, 0, CAP)
    d_tokens = jnp.einsum("tc,cd->td", full_select, pieces, precision=lax.Precision.HIGHEST)
    return (hidden, d_tokens)


def named_counts(ids, count):
    row_id = lax.broadcasted_iota(jnp.int32, (count, count), 0)
    col_id = lax.broadcasted_iota(jnp.int32, (count, count), 1)
    named_row = jnp.where((ids[0:1, :] == 0) | (ids[1:2, :] == 0), 1.0, 0.0)
    across = jnp.broadcast_to(named_row, (count, count))
    named_col = jnp.sum(jnp.where(row_id == col_id, across, 0.0), axis=1, keepdims=True)
    before_col = jnp.sum(jnp.where(col_id < row_id, across, 0.0), axis=1, keepdims=True)
    down = jnp.broadcast_to(named_col, (count, count))
    before_row = jnp.sum(jnp.where(row_id < col_id, down, 0.0), axis=0, keepdims=True)
    return named_row, before_row, named_col, before_col


def place_kernel(ids, slots, hid_in, dtok, hid_out):
    count = dtok.shape[0]
    hid_out[...] = hid_in[...]
    _, _, named_col, before_col = named_counts(ids, count)
    lane = lax.broadcasted_iota(jnp.int32, (count, 2 * UNIT), 1).astype(jnp.float32)
    placed = jnp.where((before_col == lane) & (named_col == 1.0), 1.0, 0.0)
    dtok[...] = jnp.dot(
        placed, slots[...].reshape(2 * UNIT, dtok.shape[1]),
        precision=lax.Precision.HIGHEST, preferred_element_type=jnp.float32)


def expert_kernel(nz, ny, tok, ids, gate, up, dh, hid, slots,
                  tokv, own, oth, wg, wu, accg, accu, dhv, dgv, duv, hst,
                  csend, crecv, full, keep, ysend, yrecv, zsend, zrecv, fin, xsend, xrecv,
                  load_sem, send_sem, recv_sem):
    pipe, expert = lax.axis_index("pipe"), lax.axis_index("expert")
    x, c = pipe // CORES, lax.rem(pipe, CORES)
    z, y = expert // ny, lax.rem(expert, ny)
    half_steps = STEPS // 2
    width = tokv.shape[2]
    half = wg.shape[3]
    count = tok.shape[0]
    span = width * half_steps
    ring = range(1, nz)
    z_to = {d: lax.rem(z + d, nz) for d in ring}
    z_from = {d: lax.rem(z + nz - d, nz) for d in ring}
    core_peer = (x * CORES + 1 - c, expert)
    x_peer = ((1 - x) * CORES + c, expert)
    y_peer = (pipe, z * ny + 1 - y)
    z_peer = {d: (pipe, z_to[d] * ny + y) for d in ring}

    taken = [0, 0]

    def load(src, dst):
        taken[0] += 1
        copy = pltpu.make_async_copy(src, dst, load_sem.at[taken[0] - 1])
        copy.start()
        return copy

    def send(src, dst, device):
        taken[1] += 1
        index = taken[1] - 1
        copy = pltpu.make_async_remote_copy(
            src_ref=src, dst_ref=dst, send_sem=send_sem.at[index], recv_sem=recv_sem.at[index],
            device_id=device, device_id_type=MESH_ID)
        copy.start()
        sent.append(copy)
        return copy

    sent = []

    def offset(other, s):
        part = c if other == 0 else 1 - c
        where = 1 - x if s < half_steps else x
        return pl.multiple_of((where * CORES + part) * span + (s % half_steps) * width, 128)

    barrier = pltpu.get_barrier_semaphore()
    peers = [core_peer, x_peer, y_peer] + [z_peer[d] for d in ring]
    for peer in peers:
        pl.semaphore_signal(barrier, inc=1, device_id=peer, device_id_type=MESH_ID)

    mine = pl.ds(pl.multiple_of(c * half, 128), half)
    others = pl.ds(pl.multiple_of((1 - c) * half, 128), half)
    tok_loads = [load(tok.at[:, pl.ds(offset(0, s), width)], tokv.at[s]) for s in range(STEPS)]
    w_loads = {}
    for s in range(STEPS):
        for other in (0, 1):
            rows = pl.ds(offset(other, s), width)
            w_loads[other, s] = (
                load(gate.at[rows, mine], wg.at[other, s]), load(up.at[rows, mine], wu.at[other, s]))
    dh_load = load(dh.at[:, mine], dhv.at[c])

    named_row, before_row, _, _ = named_counts(ids, count)
    slot_id = (lax.broadcasted_iota(jnp.int32, (UNIT, count), 0) + x * UNIT).astype(jnp.float32)
    select = jnp.where((before_row == slot_id) & (named_row == 1.0), 1.0, 0.0).astype(jnp.bfloat16)

    pl.semaphore_wait(barrier, len(peers))
    dh_copy = send(dh.at[:, others], dhv.at[c], core_peer)

    z_copies, y_copies, core_copies = {}, {}, {}
    for s in range(STEPS):
        tok_loads[s].wait()
        own[s, expert] = jnp.dot(
            select, tokv[s], preferred_element_type=jnp.float32).astype(jnp.bfloat16)
        for d in ring:
            z_copies[s, d] = send(own.at[s, expert], own.at[s, expert], z_peer[d])
        y_copies[s, 0] = send(own.at[s, expert], own.at[s, expert], y_peer)

    def forward(other, s):
        block = (own if other == 0 else oth)[s].reshape(nz * ny * UNIT, width)
        for copy in w_loads[other, s]:
            copy.wait()
        for acc, weight in ((accg, wg), (accu, wu)):
            term = jnp.dot(block, weight[other, s], preferred_element_type=jnp.float32)
            if other == 0 and s == 0:
                acc[...] = term
            else:
                acc[...] += term

    for i in range(STEPS + C_LAG):
        if i < STEPS:
            for d in ring:
                z_copies[i, d].wait_recv()
                place = z_from[d] * ny + y
                y_copies[i, d] = send(own.at[i, place], own.at[i, place], y_peer)
        s = i - Y_LAG
        if 0 <= s < STEPS:
            for d in range(nz):
                y_copies[s, d].wait_recv()
            core_copies[s] = send(own.at[s], oth.at[s], core_peer)
            forward(0, s)
        s = i - C_LAG
        if 0 <= s < STEPS:
            core_copies[s].wait_recv()
            forward(1, s)

    dh_load.wait()
    dh_copy.wait_recv()
    blocks = nz * ny
    tile = 256 if half % 256 == 0 else half
    for n in range(0, half, tile):
        cols = slice(n, n + tile)
        gate_value, up_value = accg[:, cols], accu[:, cols]
        first = dhv[0, :, cols].astype(jnp.float32).reshape(blocks, UNIT // 2, tile)
        second = dhv[1, :, cols].astype(jnp.float32).reshape(blocks, UNIT // 2, tile)
        upstream = jnp.stack([first, second], axis=1).reshape(blocks * UNIT, tile)
        sigmoid_gate = jax.nn.sigmoid(gate_value)
        activated = gate_value * sigmoid_gate
        hidden = (activated * up_value).reshape(blocks, 2, UNIT // 2, tile)
        for q in (0, 1):
            hst[q, :, cols] = hidden[:, q].reshape(blocks * UNIT // 2, tile).astype(jnp.bfloat16)
        dgv[:, cols] = (
            upstream * up_value * sigmoid_gate * (1.0 + gate_value * (1.0 - sigmoid_gate))
        ).astype(jnp.bfloat16)
        duv[:, cols] = (upstream * activated).astype(jnp.bfloat16)
    hid_load = load(hst.at[c], hid.at[:, mine])

    contract = (((1,), (1,)), ((), ()))

    def backward(other, s):
        return lax.dot_general(
            dgv[...], wg[other, s], contract, preferred_element_type=jnp.float32
        ) + lax.dot_general(
            duv[...], wu[other, s], contract, preferred_element_type=jnp.float32)

    core_sums, y_sums, z_sums, x_sums = {}, {}, {}, {}
    hid_copy = None
    for i in range(STEPS + Z_SUM_LAG):
        if i < STEPS:
            csend[i] = backward(1, i).astype(jnp.bfloat16)
            core_sums[i] = send(csend.at[i], crecv.at[i], core_peer)
        s = i - ADD_LAG
        if 0 <= s < STEPS:
            core_sums[s].wait_recv()
            total = crecv[s].astype(jnp.float32).reshape(blocks, UNIT, width)
            full[s % 2] = full[s % 2] + total
            for k in range(nz):
                ysend[s, k] = full[s % 2, k * ny + 1 - y].astype(jnp.bfloat16)
                keep[s, k] = full[s % 2, k * ny + y]
            y_sums[s] = send(ysend.at[s], yrecv.at[s], y_peer)
            if hid_copy is None:
                hid_copy = send(hst.at[1 - c], hid.at[:, mine], core_peer)
        if i < STEPS:
            full[i % 2] = backward(0, i).reshape(blocks, UNIT, width)
        s = i - Y_SUM_LAG
        if 0 <= s < STEPS:
            y_sums[s].wait_recv()
            for d in ring:
                zsend[s, d - 1] = (
                    keep[s, z_to[d]] + yrecv[s, z_to[d]].astype(jnp.float32)).astype(jnp.bfloat16)
                z_sums[s, d] = send(zsend.at[s, d - 1], zrecv.at[s, d - 1], z_peer[d])
            fin[s] = keep[s, z] + yrecv[s, z].astype(jnp.float32)
        s = i - Z_SUM_LAG
        if 0 <= s < STEPS:
            for d in ring:
                z_sums[s, d].wait_recv()
            done = fin[s]
            for d in ring:
                done = done + zrecv[s, d - 1].astype(jnp.float32)
            if s < half_steps:
                xsend[s] = done
                x_sums[s] = send(xsend.at[s], xrecv.at[s], x_peer)
            else:
                fin[s] = done

    for s in range(half_steps):
        cols = slice(s * width, (s + 1) * width)
        slots[x, :, cols] = fin[half_steps + s]
        x_sums[s].wait_recv()
        slots[1 - x, :, cols] = xrecv[s]

    hid_load.wait()
    hid_copy.wait_recv()
    for copy in sent:
        copy.wait_send()


def fused_body(nz, ny, tokens, expert_ids, gate_weight, up_weight, d_hidden):
    count, features = tokens.shape
    hidden_units = gate_weight.shape[1]
    rows = d_hidden.shape[0]
    width = features // (CORES * STEPS)
    half = hidden_units // CORES
    blocks = nz * ny
    half_steps = STEPS // 2
    bf, f32 = jnp.bfloat16, jnp.float32
    loads = STEPS * 5 + 2
    sends = 2 + STEPS * (nz - 1 + nz + 1) + STEPS * (2 + nz - 1) + half_steps
    hbm = pl.BlockSpec(memory_space=pl.ANY)
    vmem = pl.BlockSpec(memory_space=pltpu.VMEM)
    flops = 8 * blocks * UNIT * features * half
    ids = expert_ids.T
    staged, slots = pl.pallas_call(
        functools.partial(expert_kernel, nz, ny),
        out_shape=(
            jax.ShapeDtypeStruct((rows, hidden_units), bf),
            jax.ShapeDtypeStruct((2, UNIT, half_steps * width), f32),
        ),
        in_specs=[hbm, vmem, hbm, hbm, hbm],
        out_specs=(hbm, vmem),
        scratch_shapes=[
            pltpu.VMEM((STEPS, count, width), bf),
            pltpu.VMEM((STEPS, blocks, UNIT, width), bf),
            pltpu.VMEM((STEPS, blocks, UNIT, width), bf),
            pltpu.VMEM((2, STEPS, width, half), bf),
            pltpu.VMEM((2, STEPS, width, half), bf),
            pltpu.VMEM((blocks * UNIT, half), f32),
            pltpu.VMEM((blocks * UNIT, half), f32),
            pltpu.VMEM((2, rows, half), bf),
            pltpu.VMEM((blocks * UNIT, half), bf),
            pltpu.VMEM((blocks * UNIT, half), bf),
            pltpu.VMEM((2, rows, half), bf),
            pltpu.VMEM((STEPS, blocks * UNIT, width), bf),
            pltpu.VMEM((STEPS, blocks * UNIT, width), bf),
            pltpu.VMEM((2, blocks, UNIT, width), f32),
            pltpu.VMEM((STEPS, nz, UNIT, width), f32),
            pltpu.VMEM((STEPS, nz, UNIT, width), bf),
            pltpu.VMEM((STEPS, nz, UNIT, width), bf),
            pltpu.VMEM((STEPS, nz - 1, UNIT, width), bf),
            pltpu.VMEM((STEPS, nz - 1, UNIT, width), bf),
            pltpu.VMEM((STEPS, UNIT, width), f32),
            pltpu.VMEM((half_steps, UNIT, width), f32),
            pltpu.VMEM((half_steps, UNIT, width), f32),
            pltpu.SemaphoreType.DMA((loads,)),
            pltpu.SemaphoreType.DMA((sends,)),
            pltpu.SemaphoreType.DMA((sends,)),
        ],
        compiler_params=pltpu.CompilerParams(
            collective_id=0, has_side_effects=True, vmem_limit_bytes=56 * 1024 * 1024),
        cost_estimate=pl.CostEstimate(
            flops=flops, bytes_accessed=4 * features * half, transcendentals=0),
    )(tokens, ids, gate_weight, up_weight, d_hidden)
    d_tokens, hidden = pl.pallas_call(
        place_kernel,
        out_shape=(
            jax.ShapeDtypeStruct((count, half_steps * width), f32),
            jax.ShapeDtypeStruct((rows, hidden_units), bf),
        ),
        in_specs=[vmem, vmem, vmem],
        out_specs=(vmem, vmem),
    )(ids, slots, staged)
    return hidden, d_tokens


def split_of(mesh):
    line = mesh.devices.reshape(mesh.shape["pipe"], mesh.shape["expert"])[0]
    coords = [getattr(device, "coords", None) for device in line]
    if coords[0] is None:
        return len(line) // 2, 2
    ny = len({tuple(at)[1] for at in coords})
    return len(line) // ny, ny


def solution(mesh):
    in_specs = (
        P("expert", None),
        P("expert", None),
        P(None, "expert"),
        P(None, "expert"),
        P("pipe", "expert"),
    )
    out_specs = (P("pipe", "expert"), P("expert", "pipe"))
    nz, ny = split_of(mesh)
    fits = ny == 2 and nz > 1 and mesh.shape["pipe"] == 2 * CORES and 2 * UNIT == CAP
    body = functools.partial(fused_body, nz, ny) if fits else plain_body
    return jax.shard_map(body, mesh=mesh, in_specs=in_specs, out_specs=out_specs, check_vma=False)
```

profile of v0, /device:TPU:0, one launch (start us, length us, event | category | flops | bytes accessed | tf_op | source)
XLA Modules:
  0.0 44.9 jit_solution(16110182659739382007)
XLA Ops:
  0.6 41.4 %shard_map.68 = (bf16[64,2048]{1,0:T(8,128)(2,1)}, f32[2,16,1536]{2,1,0:T(8,128)}) custom-call(bf16[128,6144]{1,0:T(8,128)(2,1)} %tok.1, s32[2,128]{1,0:T(2,128)} %bitcast.1, bf16[6144,2048]{1,0:T(8,128)(2,1)} %gate.1, bf16[6144,2048]{1,0:T(8,128)(2,1)} %up.1, bf16[64,2048]{1,0:T(8,128)(2,1)} %dh.1), custom_call_target="tpu_custom_call" | custom-call | flops 6442450944 | bytes 25165824 | tf_op jit(solution)/shard_map/pallas_call | solution.py:285
  42.1 2.8 %shard_map.69 = (f32[128,1536]{1,0:T(8,128)}, bf16[64,2048]{1,0:T(8,128)(2,1)}) custom-call(s32[2,128]{1,0:T(2,128)} %bitcast.2, f32[2,16,1536]{2,1,0:T(8,128)} %get-tuple-element.6.slots, bf16[64,2048]{1,0:T(8,128)(2,1)} %get-tuple-element.7.hid_in), custom_call_target="tpu_custom_call" | custom-call | tf_op jit(solution)/shard_map/pallas_call | solution.py:325
where the time goes:
time: 45 us; the launch traced here: 44.9 us
  Pallas kernels  44.2 us (98%)
  between operations  0.64 us (1%)
    pallas_call x1, Pallas kernels, fused_body(): pl.pallas_call(functools.partial(expert_kernel, nz, ny), out_shape=(jax.S...  41.4 us
    pallas_call x1, Pallas kernels, fused_body(): pl.pallas_call(place_kernel, out_shape=(jax.ShapeDtypeStruct((count, half...  2.79 us

commit v1 on v0

v1 whole, which is shorter than its diff:
```python
import functools
import math

import jax
import jax.numpy as jnp
from jax import lax
from jax.experimental import pallas as pl
from jax.experimental.pallas import tpu as pltpu
from jax.sharding import PartitionSpec as P

CAP = 32
CORES = 2
UNIT = 16
STEPS = 6
MESH_ID = pl.DeviceIdType.MESH
scope = jax.named_scope


def slot_select(expert_ids, first_slot, slot_count):
    is_named = jnp.any(expert_ids == 0, axis=1).astype(jnp.int32)
    slot_before = jnp.cumsum(is_named) - is_named
    positions = first_slot + jnp.arange(slot_count, dtype=jnp.int32)
    marked = (is_named[:, None] == 1) & (slot_before[:, None] == positions[None, :])
    return marked.astype(jnp.float32)


def plain_body(tokens, expert_ids, gate_weight, up_weight, d_hidden):
    hidden_units = gate_weight.shape[1]
    slot_span = CAP // lax.axis_size("pipe")
    own_select = slot_select(expert_ids, lax.axis_index("pipe") * slot_span, slot_span)
    routed = jnp.einsum(
        "tj,td->jd", own_select.astype(jnp.bfloat16), tokens, preferred_element_type=jnp.float32
    ).astype(jnp.bfloat16)
    piece = lax.all_gather(routed, "expert", axis=0, tiled=True)
    gate_part = jnp.dot(piece, gate_weight, preferred_element_type=jnp.float32)
    up_part = jnp.dot(piece, up_weight, preferred_element_type=jnp.float32)
    joined = jnp.concatenate([gate_part, up_part], axis=1)
    gate_value = joined[:, :hidden_units]
    up_value = joined[:, hidden_units:]
    sigmoid_gate = jax.nn.sigmoid(gate_value)
    activated = gate_value * sigmoid_gate
    hidden = (activated * up_value).astype(jnp.bfloat16)
    upstream = d_hidden.astype(jnp.float32)
    d_gate = (
        upstream * up_value * sigmoid_gate * (1.0 + gate_value * (1.0 - sigmoid_gate))
    ).astype(jnp.bfloat16)
    d_up = (upstream * activated).astype(jnp.bfloat16)
    result = jnp.einsum("nh,dh->nd", d_gate, gate_weight, preferred_element_type=jnp.float32)
    slot_grads = lax.psum_scatter(
        result + jnp.einsum("nh,dh->nd", d_up, up_weight, preferred_element_type=jnp.float32),
        "expert",
        scatter_dimension=0,
        tiled=True,
    )
    pieces = lax.all_to_all(slot_grads, "pipe", split_axis=1, concat_axis=0, tiled=True)
    full_select = slot_select(expert_ids, 0, CAP)
    d_tokens = jnp.einsum("tc,cd->td", full_select, pieces, precision=lax.Precision.HIGHEST)
    return (hidden, d_tokens)


def named_counts(ids, count):
    row_id = lax.broadcasted_iota(jnp.int32, (count, count), 0)
    col_id = lax.broadcasted_iota(jnp.int32, (count, count), 1)
    named_row = jnp.where((ids[0:1, :] == 0) | (ids[1:2, :] == 0), 1.0, 0.0)
    across = jnp.broadcast_to(named_row, (count, count))
    named_col = jnp.sum(jnp.where(row_id == col_id, across, 0.0), axis=1, keepdims=True)
    before_col = jnp.sum(jnp.where(col_id < row_id, across, 0.0), axis=1, keepdims=True)
    down = jnp.broadcast_to(named_col, (count, count))
    before_row = jnp.sum(jnp.where(row_id < col_id, down, 0.0), axis=0, keepdims=True)
    return named_row, before_row, named_col, before_col


def place_kernel(placed, slots, hid_in, dtok, hid_out, rows_out, copy_sem):
    groups, unit, features = slots.shape
    tile = rows_out.shape[2]
    hid_copy = pltpu.make_async_copy(hid_in, hid_out, copy_sem.at[0])
    hid_copy.start()
    copies = [hid_copy]
    for n in range(features // tile):
        cols = slice(n * tile, (n + 1) * tile)
        rows_out[n] = jnp.dot(
            placed[...], slots[:, :, cols].reshape(groups * unit, tile),
            precision=lax.Precision.HIGHEST, preferred_element_type=jnp.float32)
        copy = pltpu.make_async_copy(rows_out.at[n], dtok.at[:, cols], copy_sem.at[n + 1])
        copy.start()
        copies.append(copy)
    for copy in copies:
        copy.wait()


def flip(value, bit):
    return value + bit - 2 * bit * lax.rem(value // bit, 2)


def expert_kernel(nz, ny, tok, ids, gate, up, dh, hid, slots, placed,
                  tokv, own, oth, w, wt, acc, dhv, dgv, duv, hst,
                  csend, crecv, full, keep, ysend, yrecv, zsend, zrecv, fin, xsend,
                  zsend_f, zrecv_f, keep_f, ysend_f, yrecv_f,
                  load_sem, send_sem, recv_sem):
    pipe, expert = lax.axis_index("pipe"), lax.axis_index("expert")
    x, c = pipe // CORES, lax.rem(pipe, CORES)
    z, y = expert // ny, lax.rem(expert, ny)
    half_steps = STEPS // 2
    lead = half_steps
    width = tokv.shape[2]
    half = w.shape[4]
    count = tok.shape[0]
    blocks = nz * ny
    span = width * half_steps
    ring = range(1, nz)
    z_pair = {}
    for d in ring:
        other_z = z
        for k in range(nz.bit_length() - 1):
            if d >> k & 1:
                other_z = flip(other_z, 1 << k)
        z_pair[d] = other_z
    core_peer = (x * CORES + 1 - c, expert)
    x_peer = ((1 - x) * CORES + c, expert)
    y_peer = (pipe, z * ny + 1 - y)
    z_peer = {d: (pipe, z_pair[d] * ny + y) for d in ring}

    marks = {"load": {}, "recv": {}}
    sent_bytes = [0]

    def mark(kind, key):
        return marks[kind].setdefault(key, len(marks[kind]))

    def load(key, src, dst):
        pltpu.make_async_copy(src, dst, load_sem.at[mark("load", key)]).start()

    def loaded(key, ref):
        pltpu.make_async_copy(ref, ref, load_sem.at[marks["load"][key]]).wait()

    def send(key, src, dst, device):
        pltpu.make_async_remote_copy(
            src_ref=src, dst_ref=dst, send_sem=send_sem.at[0], recv_sem=recv_sem.at[mark("recv", key)],
            device_id=device, device_id_type=MESH_ID).start()
        sent_bytes[0] += math.prod(src.shape) * src.dtype.itemsize

    def landed(key, ref):
        with scope("_".join(str(k) for k in key)):
            pltpu.make_async_copy(ref, ref, recv_sem.at[marks["recv"][key]]).wait()

    def offset(other, s):
        part = c if other == 0 else 1 - c
        where = 1 - x if s < half_steps else x
        return pl.multiple_of((where * CORES + part) * span + (s % half_steps) * width, 128)

    barrier = pltpu.get_barrier_semaphore()
    peers = [core_peer, x_peer, y_peer] + [z_peer[d] for d in ring]
    for peer in peers:
        pl.semaphore_signal(barrier, inc=1, device_id=peer, device_id_type=MESH_ID)

    mine = pl.ds(pl.multiple_of(c * half, 128), half)
    others = pl.ds(pl.multiple_of((1 - c) * half, 128), half)
    for s in range(STEPS):
        load(("tok", s), tok.at[:, pl.ds(offset(0, s), width)], tokv.at[s])

    named_row, before_row, named_col, before_col = named_counts(ids, count)
    slot_id = (lax.broadcasted_iota(jnp.int32, (UNIT, count), 0) + x * UNIT).astype(jnp.float32)
    select = jnp.where((before_row == slot_id) & (named_row == 1.0), 1.0, 0.0).astype(jnp.bfloat16)

    def load_weights(s):
        for other in (0, 1):
            rows = pl.ds(offset(other, s), width)
            load(("w", s), gate.at[rows, mine], w.at[s, other, 0])
            load(("w", s), up.at[rows, mine], w.at[s, other, 1])

    weight_order = [0, lead] + [s for s in range(STEPS) if s not in (0, lead)]
    for s in weight_order[:2]:
        load_weights(s)
    with scope("barrier"):
        pl.semaphore_wait(barrier, len(peers))

    for s in range(STEPS):
        loaded(("tok", s), tokv.at[s])
        own[s, expert] = jnp.dot(
            select, tokv[s], preferred_element_type=jnp.float32).astype(jnp.bfloat16)
        for d in ring:
            send(("zin", s), own.at[s, expert], own.at[s, expert], z_peer[d])
        send(("yin", s), own.at[s, expert], own.at[s, expert], y_peer)
        if s + 2 < STEPS:
            load_weights(weight_order[s + 2])
    load(("dh",), dh.at[:, mine], dhv.at[c])
    send(("dhin",), dh.at[:, others], dhv.at[c], core_peer)
    lane = lax.broadcasted_iota(jnp.int32, (count, CORES * UNIT), 1).astype(jnp.float32)
    placed[...] = jnp.where((before_col == lane) & (named_col == 1.0), 1.0, 0.0)

    waited, turned = set(), set()

    def weights_in(s):
        if s not in waited:
            waited.add(s)
            with scope(f"w{s}"):
                loaded(("w", s), w.at[s])

    def turn(other, s, mats=(0, 1)):
        weights_in(s)
        turned.add((other, s))
        with scope(f"turn{other}{s}"):
            for m in mats:
                wt[s, other, m] = w[s, other, m].T

    def relay(s):
        landed(("zin", s), own.at[s, pl.ds(0, nz - 1)])
        for d in ring:
            place = z_pair[d] * ny + y
            send(("yin", s), own.at[s, place], own.at[s, place], y_peer)

    def share(s):
        landed(("yin", s), own.at[s, pl.ds(0, nz)])
        send(("cin", s), own.at[s], oth.at[s], core_peer)

    started = []

    def forward(other, s, also=()):
        weights_in(s)
        if other == 1:
            landed(("cin", s), oth.at[s])
        for _, t in also:
            weights_in(t)
        turned.update(also)
        with scope(f"fwd{other}{s}"):
            block = (own if other == 0 else oth)[s].reshape(blocks * UNIT, width)
            for m in (0, 1):
                for o, t in also:
                    wt[t, o, m] = w[t, o, m].T
                term = jnp.dot(block, w[s, other, m], preferred_element_type=jnp.float32)
                if started:
                    acc[m] += term
                else:
                    acc[m] = term
            started.append(s)

    turn(0, 0)
    turn(1, 0)
    turn(0, 3)
    turn(1, 3, [0])
    relay(0)
    turn(1, 3, [1])
    relay(1)
    turn(1, 1, [0])
    relay(2)
    share(0)
    turn(1, 1, [1])
    relay(3)
    share(1)
    forward(0, 0, [(0, 1)])
    relay(4)
    share(2)
    forward(1, 0, [(1, 2)])
    relay(5)
    share(3)
    forward(0, 1, [(1, 4)])
    forward(1, 1, [(0, 2)])
    share(4)
    forward(0, 2, [(1, 5)])
    forward(1, 2, [(0, 4)])
    forward(0, 3)
    share(5)
    forward(1, 3)
    forward(0, 4, [(0, 5)])
    forward(1, 4)
    forward(0, 5)
    forward(1, 5)

    loaded(("dh",), dhv.at[0])
    landed(("dhin",), dhv.at[0])
    tile = 256 if half % 256 == 0 else half
    with scope("epilogue"):
        for n in range(0, half, tile):
            cols = slice(n, n + tile)
            gate_value, up_value = acc[0, :, cols], acc[1, :, cols]
            first = dhv[0, :, cols].astype(jnp.float32).reshape(blocks, UNIT // 2, tile)
            second = dhv[1, :, cols].astype(jnp.float32).reshape(blocks, UNIT // 2, tile)
            upstream = jnp.stack([first, second], axis=1).reshape(blocks * UNIT, tile)
            sigmoid_gate = jax.nn.sigmoid(gate_value)
            activated = gate_value * sigmoid_gate
            hidden = (activated * up_value).reshape(blocks, 2, UNIT // 2, tile)
            for q in (0, 1):
                hst[q, :, cols] = hidden[:, q].reshape(blocks * UNIT // 2, tile).astype(jnp.bfloat16)
            dgv[:, cols] = (
                upstream * up_value * sigmoid_gate * (1.0 + gate_value * (1.0 - sigmoid_gate))
            ).astype(jnp.bfloat16)
            duv[:, cols] = (upstream * activated).astype(jnp.bfloat16)
    load(("hid",), hst.at[c], hid.at[:, mine])

    def backward(other, s):
        if (other, s) in turned:
            return jnp.dot(
                dgv[...], wt[s, other, 0], preferred_element_type=jnp.float32
            ) + jnp.dot(duv[...], wt[s, other, 1], preferred_element_type=jnp.float32)
        contract = (((1,), (1,)), ((), ()))
        return lax.dot_general(
            dgv[...], w[s, other, 0], contract, preferred_element_type=jnp.float32
        ) + lax.dot_general(duv[...], w[s, other, 1], contract, preferred_element_type=jnp.float32)

    turn_of = {}

    def back_other(s):
        turn_of[s] = len(turn_of) % 2
        with scope(f"bwd1{s}"):
            csend[s] = backward(1, s).astype(jnp.bfloat16)
        send(("csum", s), csend.at[s], crecv.at[s], core_peer)

    def back_own(s):
        with scope(f"bwd0{s}"):
            full[turn_of[s]] = backward(0, s).reshape(blocks, UNIT, width)

    def core_add(s):
        landed(("csum", s), crecv.at[s])
        with scope(f"cadd{s}"):
            side = turn_of[s]
            full[side] = full[side] + crecv[s].astype(jnp.float32).reshape(blocks, UNIT, width)
            if s == lead:
                for d in ring:
                    zsend_f[d - 1] = full[side, pl.ds(z_pair[d] * ny, ny)].astype(jnp.bfloat16)
                    send(("zsum", s), zsend_f.at[d - 1], zrecv_f.at[d - 1], z_peer[d])
                keep_f[...] = full[side, pl.ds(z * ny, ny)]
            else:
                for d in [*ring, 0]:
                    place = (z_pair[d] if d else z) * ny
                    ysend[s, d] = full[side, place + 1 - y].astype(jnp.bfloat16)
                    send(("ysum", s, d), ysend.at[s, d], yrecv.at[s, d], y_peer)
                for d in [*ring, 0]:
                    keep[s, d] = full[side, (z_pair[d] if d else z) * ny + y]

    def lead_add():
        landed(("zsum", lead), zrecv_f)
        total = keep_f[...]
        for d in ring:
            total = total + zrecv_f[d - 1].astype(jnp.float32)
        keep_f[...] = total
        ysend_f[...] = keep_f[1 - y].astype(jnp.bfloat16)
        send(("ysum", lead), ysend_f, yrecv_f, y_peer)

    def y_add(s):
        for d in ring:
            landed(("ysum", s, d), yrecv.at[s, d])
            zsend[s, d - 1] = (keep[s, d] + yrecv[s, d].astype(jnp.float32)).astype(jnp.bfloat16)
            send(("zsum", s), zsend.at[s, d - 1], zrecv.at[s, d - 1], z_peer[d])

    def finish(s):
        if s == lead:
            landed(("ysum", s), yrecv_f)
            done = keep_f[y] + yrecv_f[...].astype(jnp.float32)
        else:
            landed(("ysum", s, 0), yrecv.at[s, 0])
            fin[s] = keep[s, 0] + yrecv[s, 0].astype(jnp.float32)
            landed(("zsum", s), zrecv.at[s])
            done = fin[s]
            for d in ring:
                done = done + zrecv[s, d - 1].astype(jnp.float32)
        cols = slice((s % half_steps) * width, (s % half_steps + 1) * width)
        if s < half_steps:
            xsend[s] = done
            send(("xsum",), xsend.at[s], slots.at[x, :, cols], x_peer)
        else:
            slots[x, :, cols] = done

    back_other(0)
    back_own(0)
    back_other(3)
    core_add(0)
    send(("hidin",), hst.at[1 - c], hid.at[:, mine], core_peer)
    back_own(3)
    back_other(1)
    core_add(3)
    back_own(1)
    back_other(2)
    core_add(1)
    back_own(2)
    back_other(4)
    core_add(2)
    y_add(0)
    back_own(4)
    back_other(5)
    core_add(4)
    back_own(5)
    y_add(1)
    core_add(5)
    y_add(2)
    lead_add()
    y_add(4)
    finish(0)
    y_add(5)
    finish(1)
    finish(2)
    finish(3)
    finish(4)
    finish(5)

    landed(("xsum",), slots.at[0])
    loaded(("hid",), hst.at[0])
    landed(("hidin",), hst.at[0])
    with scope("sent"):
        every = w.reshape(2 * CORES * STEPS * width, half)
        rows_sent = sent_bytes[0] // (half * w.dtype.itemsize)
        pltpu.make_async_copy(every.at[pl.ds(0, rows_sent)], every.at[pl.ds(0, rows_sent)], send_sem.at[0]).wait()


def fused_body(nz, ny, tokens, expert_ids, gate_weight, up_weight, d_hidden):
    count, features = tokens.shape
    hidden_units = gate_weight.shape[1]
    rows = d_hidden.shape[0]
    width = features // (CORES * STEPS)
    half = hidden_units // CORES
    blocks = nz * ny
    half_steps = STEPS // 2
    bf, f32 = jnp.bfloat16, jnp.float32
    loads = STEPS * 2 + 2
    recvs = STEPS * 4 + (STEPS - 1) * nz + 1 + STEPS + 3
    hbm = pl.BlockSpec(memory_space=pl.ANY)
    vmem = pl.BlockSpec(memory_space=pltpu.VMEM)
    flops = 8 * blocks * UNIT * features * half
    ids = expert_ids.T
    staged, slots, placed = pl.pallas_call(
        functools.partial(expert_kernel, nz, ny),
        out_shape=(
            pltpu.VMEM((rows, hidden_units), bf),
            pltpu.VMEM((CORES, UNIT, half_steps * width), f32),
            pltpu.VMEM((count, CORES * UNIT), f32),
        ),
        in_specs=[hbm, vmem, hbm, hbm, hbm],
        out_specs=(vmem, vmem, vmem),
        scratch_shapes=[
            pltpu.VMEM((STEPS, count, width), bf),
            pltpu.VMEM((STEPS, blocks, UNIT, width), bf),
            pltpu.VMEM((STEPS, blocks, UNIT, width), bf),
            pltpu.VMEM((STEPS, 2, 2, width, half), bf),
            pltpu.VMEM((STEPS, 2, 2, half, width), bf),
            pltpu.VMEM((2, blocks * UNIT, half), f32),
            pltpu.VMEM((2, rows, half), bf),
            pltpu.VMEM((blocks * UNIT, half), bf),
            pltpu.VMEM((blocks * UNIT, half), bf),
            pltpu.VMEM((2, rows, half), bf),
            pltpu.VMEM((STEPS, blocks * UNIT, width), bf),
            pltpu.VMEM((STEPS, blocks * UNIT, width), bf),
            pltpu.VMEM((2, blocks, UNIT, width), f32),
            pltpu.VMEM((STEPS, nz, UNIT, width), f32),
            pltpu.VMEM((STEPS, nz, UNIT, width), bf),
            pltpu.VMEM((STEPS, nz, UNIT, width), bf),
            pltpu.VMEM((STEPS, nz - 1, UNIT, width), bf),
            pltpu.VMEM((STEPS, nz - 1, UNIT, width), bf),
            pltpu.VMEM((STEPS, UNIT, width), f32),
            pltpu.VMEM((half_steps, UNIT, width), f32),
            pltpu.VMEM((nz - 1, ny, UNIT, width), bf),
            pltpu.VMEM((nz - 1, ny, UNIT, width), bf),
            pltpu.VMEM((ny, UNIT, width), f32),
            pltpu.VMEM((UNIT, width), bf),
            pltpu.VMEM((UNIT, width), bf),
            pltpu.SemaphoreType.DMA((loads,)),
            pltpu.SemaphoreType.DMA((1,)),
            pltpu.SemaphoreType.DMA((recvs,)),
        ],
        compiler_params=pltpu.CompilerParams(
            collective_id=0, has_side_effects=True, vmem_limit_bytes=62 * 1024 * 1024),
        cost_estimate=pl.CostEstimate(
            flops=flops, bytes_accessed=4 * features * half, transcendentals=0),
    )(tokens, ids, gate_weight, up_weight, d_hidden)
    d_tokens, hidden = pl.pallas_call(
        place_kernel,
        out_shape=(
            jax.ShapeDtypeStruct((count, half_steps * width), f32),
            jax.ShapeDtypeStruct((rows, hidden_units), bf),
        ),
        in_specs=[vmem, vmem, vmem],
        out_specs=(hbm, hbm),
        scratch_shapes=[
            pltpu.VMEM((half_steps, count, width), f32),
            pltpu.SemaphoreType.DMA((half_steps + 1,)),
        ],
    )(*[pltpu.with_memory_space_constraint(v, pltpu.VMEM) for v in (placed, slots, staged)])
    return hidden, d_tokens


def split_of(mesh):
    line = mesh.devices.reshape(mesh.shape["pipe"], mesh.shape["expert"])[0]
    coords = [getattr(device, "coords", None) for device in line]
    if coords[0] is None:
        return len(line) // 2, 2
    ny = len({tuple(at)[1] for at in coords})
    return len(line) // ny, ny


def solution(mesh):
    in_specs = (
        P("expert", None),
        P("expert", None),
        P(None, "expert"),
        P(None, "expert"),
        P("pipe", "expert"),
    )
    out_specs = (P("pipe", "expert"), P("expert", "pipe"))
    nz, ny = split_of(mesh)
    fits = ny == 2 and nz in (2, 4) and mesh.shape["pipe"] == 2 * CORES and 2 * UNIT == CAP
    body = functools.partial(fused_body, nz, ny) if fits else plain_body
    return jax.shard_map(body, mesh=mesh, in_specs=in_specs, out_specs=out_specs, check_vma=False)
```

time: 45 us -> 42.4 us (0.942)
  Pallas kernels: 44.2 us -> 41.4 us
    pallas_call x1, Pallas kernels: 41.4 us -> 39.9 us  [fused_body(): pl.pallas_call(functools.partial(expert_kernel, nz, ny), out_shape=(pltpu...]
    pallas_call x1, Pallas kernels: 2.79 us -> 1.49 us  [fused_body(): pl.pallas_call(place_kernel, out_shape=(jax.ShapeDtypeStruct((count, half...]
where the time goes in v1:
time: 42.4 us; the launch traced here: 42.2 us
  Pallas kernels  41.4 us (98%)
  between operations  0.8 us (2%)
    pallas_call x1, Pallas kernels, fused_body(): pl.pallas_call(functools.partial(expert_kernel, nz, ny), out_shape=(pltpu...  39.9 us
    pallas_call x1, Pallas kernels, fused_body(): pl.pallas_call(place_kernel, out_shape=(jax.ShapeDtypeStruct((count, half...  1.49 us

profile of v1, /device:TPU:0, one launch (start us, length us, event | category | flops | bytes accessed | tf_op | source)
XLA Modules:
  0.0 42.2 jit_solution(9206866430873263547)
XLA Ops:
  0.6 39.9 %shard_map.68 = (bf16[64,2048]{1,0:T(8,128)(2,1)S(1)}, f32[2,16,1536]{2,1,0:T(8,128)S(1)}, f32[128,32]{1,0:T(8,128)S(1)}) custom-call(bf16[128,6144]{1,0:T(8,128)(2,1)} %tok.1, s32[2,128]{1,0:T(2,128)} %bitcast.1, bf16[6144,2048]{1,0:T(8,128)(2,1)} %gate.1, bf16[6144,2048]{1,0:T(8,128)(2,1)} %up.1, bf16[64,2048]{1,0:T(8,128)(2,1)} %dh.1), custom_call_target="tpu_custom_call" | custom-call | flops 6442450944 | bytes 25165824 | tf_op jit(solution)/shard_map/pallas_call | solution.py:418
  40.5 1.5 %shard_map.69 = (f32[128,1536]{1,0:T(8,128)}, bf16[64,2048]{1,0:T(8,128)(2,1)}) custom-call(f32[128,32]{1,0:T(8,128)S(1)} %get-tuple-element.7.placed, f32[2,16,1536]{2,1,0:T(8,128)S(1)} %get-tuple-element.8.slots, bf16[64,2048]{1,0:T(8,128)(2,1)S(1)} %get-tuple-element.9.hid_in), custom_call_target="tpu_custom_call" | custom-call | tf_op jit(solution)/shard_map/pallas_call | solution.py:462

commit v2 on v1

--- a/solution.py
+++ b/solution.py
@@ -175,11 +175,11 @@
 
     for s in range(STEPS):
         loaded(("tok", s), tokv.at[s])
-        own[s, expert] = jnp.dot(
+        own[s, z, y] = jnp.dot(
             select, tokv[s], preferred_element_type=jnp.float32).astype(jnp.bfloat16)
         for d in ring:
-            send(("zin", s), own.at[s, expert], own.at[s, expert], z_peer[d])
-        send(("yin", s), own.at[s, expert], own.at[s, expert], y_peer)
+            send(("zin", s), own.at[s, z, y], own.at[s, z, y], z_peer[d])
+        send(("yin", s), own.at[s, z, y], own.at[s, z, y], y_peer)
         if s + 2 < STEPS:
             load_weights(weight_order[s + 2])
     load(("dh",), dh.at[:, mine], dhv.at[c])
@@ -203,14 +203,15 @@
                 wt[s, other, m] = w[s, other, m].T
 
     def relay(s):
-        landed(("zin", s), own.at[s, pl.ds(0, nz - 1)])
+        landed(("zin", s), own.at[s, pl.ds(0, nz - 1), 0])
         for d in ring:
-            place = z_pair[d] * ny + y
-            send(("yin", s), own.at[s, place], own.at[s, place], y_peer)
+            piece = own.at[s, z_pair[d], y]
+            send(("yin", s), piece, piece, y_peer)
+        send(("cin", s), own.at[s, :, y], oth.at[s, :, y], core_peer)
 
     def share(s):
-        landed(("yin", s), own.at[s, pl.ds(0, nz)])
-        send(("cin", s), own.at[s], oth.at[s], core_peer)
+        landed(("yin", s), own.at[s, :, 0])
+        send(("cin", s), own.at[s, :, 1 - y], oth.at[s, :, 1 - y], core_peer)
 
     started = []
 
@@ -236,31 +237,34 @@
     turn(0, 0)
     turn(1, 0)
     turn(0, 3)
-    turn(1, 3, [0])
+    turn(1, 3)
     relay(0)
-    turn(1, 3, [1])
+    turn(1, 1)
     relay(1)
-    turn(1, 1, [0])
+    turn(0, 1)
+    turn(1, 2)
     relay(2)
+    turn(0, 2)
+    relay(3)
+    turn(1, 4, [0])
+    relay(4)
+    turn(1, 4, [1])
     share(0)
-    turn(1, 1, [1])
-    relay(3)
+    relay(5)
+    forward(0, 0)
     share(1)
-    forward(0, 0, [(0, 1)])
-    relay(4)
+    forward(0, 1)
     share(2)
-    forward(1, 0, [(1, 2)])
-    relay(5)
+    forward(0, 2)
+    forward(1, 0)
     share(3)
-    forward(0, 1, [(1, 4)])
-    forward(1, 1, [(0, 2)])
+    forward(1, 1)
+    forward(0, 3)
     share(4)
-    forward(0, 2, [(1, 5)])
-    forward(1, 2, [(0, 4)])
-    forward(0, 3)
+    forward(1, 2)
+    forward(0, 4)
     share(5)
     forward(1, 3)
-    forward(0, 4, [(0, 5)])
     forward(1, 4)
     forward(0, 5)
     forward(1, 5)
@@ -301,30 +305,34 @@
     def back_other(s):
         turn_of[s] = len(turn_of) % 2
         with scope(f"bwd1{s}"):
-            csend[s] = backward(1, s).astype(jnp.bfloat16)
-        send(("csum", s), csend.at[s], crecv.at[s], core_peer)
+            csend[s] = backward(1, s).reshape(nz, ny, UNIT, width).astype(jnp.bfloat16)
+        for n in (1 - y, y):
+            send(("csum", s, n is y), csend.at[s, :, n], crecv.at[s, :, n], core_peer)
 
     def back_own(s):
         with scope(f"bwd0{s}"):
-            full[turn_of[s]] = backward(0, s).reshape(blocks, UNIT, width)
+            full[turn_of[s]] = backward(0, s).reshape(nz, ny, UNIT, width)
+
+    def core_sum(s, where):
+        return full[turn_of[s], where[0], where[1]] + crecv[s, where[0], where[1]].astype(jnp.float32)
 
     def core_add(s):
-        landed(("csum", s), crecv.at[s])
-        with scope(f"cadd{s}"):
-            side = turn_of[s]
-            full[side] = full[side] + crecv[s].astype(jnp.float32).reshape(blocks, UNIT, width)
-            if s == lead:
-                for d in ring:
-                    zsend_f[d - 1] = full[side, pl.ds(z_pair[d] * ny, ny)].astype(jnp.bfloat16)
-                    send(("zsum", s), zsend_f.at[d - 1], zrecv_f.at[d - 1], z_peer[d])
-                keep_f[...] = full[side, pl.ds(z * ny, ny)]
-            else:
-                for d in [*ring, 0]:
-                    place = (z_pair[d] if d else z) * ny
-                    ysend[s, d] = full[side, place + 1 - y].astype(jnp.bfloat16)
-                    send(("ysum", s, d), ysend.at[s, d], yrecv.at[s, d], y_peer)
-                for d in [*ring, 0]:
-                    keep[s, d] = full[side, (z_pair[d] if d else z) * ny + y]
+        landed(("csum", s, False), crecv.at[s, :, 0])
+        if s == lead:
+            landed(("csum", s, True), crecv.at[s, :, 0])
+            for d in ring:
+                for n in range(ny):
+                    zsend_f[d - 1, n] = core_sum(s, (z_pair[d], n)).astype(jnp.bfloat16)
+                send(("zsum", s), zsend_f.at[d - 1], zrecv_f.at[d - 1], z_peer[d])
+            for n in range(ny):
+                keep_f[n] = core_sum(s, (z, n))
+        else:
+            for d in [*ring, 0]:
+                ysend[s, d] = core_sum(s, (z_pair[d] if d else z, 1 - y)).astype(jnp.bfloat16)
+                send(("ysum", s, d), ysend.at[s, d], yrecv.at[s, d], y_peer)
+            landed(("csum", s, True), crecv.at[s, :, 0])
+            for d in [*ring, 0]:
+                keep[s, d] = core_sum(s, (z_pair[d] if d else z, y))
 
     def lead_add():
         landed(("zsum", lead), zrecv_f)
@@ -410,7 +418,7 @@
     half_steps = STEPS // 2
     bf, f32 = jnp.bfloat16, jnp.float32
     loads = STEPS * 2 + 2
-    recvs = STEPS * 4 + (STEPS - 1) * nz + 1 + STEPS + 3
+    recvs = STEPS * 5 + (STEPS - 1) * nz + 1 + STEPS + 3
     hbm = pl.BlockSpec(memory_space=pl.ANY)
     vmem = pl.BlockSpec(memory_space=pltpu.VMEM)
     flops = 8 * blocks * UNIT * features * half
@@ -426,8 +434,8 @@
         out_specs=(vmem, vmem, vmem),
         scratch_shapes=[
             pltpu.VMEM((STEPS, count, width), bf),
-            pltpu.VMEM((STEPS, blocks, UNIT, width), bf),
-            pltpu.VMEM((STEPS, blocks, UNIT, width), bf),
+            pltpu.VMEM((STEPS, nz, ny, UNIT, width), bf),
+            pltpu.VMEM((STEPS, nz, ny, UNIT, width), bf),
             pltpu.VMEM((STEPS, 2, 2, width, half), bf),
             pltpu.VMEM((STEPS, 2, 2, half, width), bf),
             pltpu.VMEM((2, blocks * UNIT, half), f32),
@@ -435,9 +443,9 @@
             pltpu.VMEM((blocks * UNIT, half), bf),
             pltpu.VMEM((blocks * UNIT, half), bf),
             pltpu.VMEM((2, rows, half), bf),
-            pltpu.VMEM((STEPS, blocks * UNIT, width), bf),
-            pltpu.VMEM((STEPS, blocks * UNIT, width), bf),
-            pltpu.VMEM((2, blocks, UNIT, width), f32),
+            pltpu.VMEM((STEPS, nz, ny, UNIT, width), bf),
+            pltpu.VMEM((STEPS, nz, ny, UNIT, width), bf),
+            pltpu.VMEM((2, nz, ny, UNIT, width), f32),
             pltpu.VMEM((STEPS, nz, UNIT, width), f32),
             pltpu.VMEM((STEPS, nz, UNIT, width), bf),
             pltpu.VMEM((STEPS, nz, UNIT, width), bf),

time: 42.4 us -> 40.7 us (0.960)
  Pallas kernels: 41.4 us -> 39.7 us
    pallas_call x1, Pallas kernels: 39.9 us -> 38.2 us  [fused_body(): pl.pallas_call(functools.partial(expert_kernel, nz, ny), out_shape=(pltpu...]
where the time goes in v2:
time: 40.7 us; the launch traced here: 40.5 us
  Pallas kernels  39.7 us (98%)
  between operations  0.8 us (2%)
    pallas_call x1, Pallas kernels, fused_body(): pl.pallas_call(functools.partial(expert_kernel, nz, ny), out_shape=(pltpu...  38.2 us
    pallas_call x1, Pallas kernels, fused_body(): pl.pallas_call(place_kernel, out_shape=(jax.ShapeDtypeStruct((count, half...  1.5 us

profile of v2, /device:TPU:0, one launch (start us, length us, event | category | flops | bytes accessed | tf_op | source)
XLA Modules:
  0.0 40.5 jit_solution(6688072087682246933)
XLA Ops:
  0.6 38.2 %shard_map.68 = (bf16[64,2048]{1,0:T(8,128)(2,1)S(1)}, f32[2,16,1536]{2,1,0:T(8,128)S(1)}, f32[128,32]{1,0:T(8,128)S(1)}) custom-call(bf16[128,6144]{1,0:T(8,128)(2,1)} %tok.1, s32[2,128]{1,0:T(2,128)} %bitcast.1, bf16[6144,2048]{1,0:T(8,128)(2,1)} %gate.1, bf16[6144,2048]{1,0:T(8,128)(2,1)} %up.1, bf16[64,2048]{1,0:T(8,128)(2,1)} %dh.1), custom_call_target="tpu_custom_call" | custom-call | flops 6442450944 | bytes 25165824 | tf_op jit(solution)/shard_map/pallas_call | solution.py:426
  38.9 1.5 %shard_map.69 = (f32[128,1536]{1,0:T(8,128)}, bf16[64,2048]{1,0:T(8,128)(2,1)}) custom-call(f32[128,32]{1,0:T(8,128)S(1)} %get-tuple-element.7.placed, f32[2,16,1536]{2,1,0:T(8,128)S(1)} %get-tuple-element.8.slots, bf16[64,2048]{1,0:T(8,128)(2,1)S(1)} %get-tuple-element.9.hid_in), custom_call_target="tpu_custom_call" | custom-call | tf_op jit(solution)/shard_map/pallas_call | solution.py:470

commit v3 on v2

--- a/solution.py
+++ b/solution.py
@@ -76,11 +76,16 @@
     hid_copy = pltpu.make_async_copy(hid_in, hid_out, copy_sem.at[0])
     hid_copy.start()
     copies = [hid_copy]
+    chosen = jnp.concatenate([placed[...].astype(jnp.bfloat16)] * 3, axis=1)
     for n in range(features // tile):
         cols = slice(n * tile, (n + 1) * tile)
+        rest = slots[:, :, cols].reshape(groups * unit, tile)
+        parts = []
+        for _ in range(3):
+            parts.append(rest.astype(jnp.bfloat16))
+            rest = rest - parts[-1].astype(jnp.float32)
         rows_out[n] = jnp.dot(
-            placed[...], slots[:, :, cols].reshape(groups * unit, tile),
-            precision=lax.Precision.HIGHEST, preferred_element_type=jnp.float32)
+            chosen, jnp.concatenate(parts, axis=0), preferred_element_type=jnp.float32)
         copy = pltpu.make_async_copy(rows_out.at[n], dtok.at[:, cols], copy_sem.at[n + 1])
         copy.start()
         copies.append(copy)
@@ -88,13 +93,9 @@
         copy.wait()
 
 
-def flip(value, bit):
-    return value + bit - 2 * bit * lax.rem(value // bit, 2)
-
-
 def expert_kernel(nz, ny, tok, ids, gate, up, dh, hid, slots, placed,
                   tokv, own, oth, w, wt, acc, dhv, dgv, duv, hst,
-                  csend, crecv, full, keep, ysend, yrecv, zsend, zrecv, fin, xsend,
+                  csend, crecv, full, keep, ysend, yrecv, zsend, zrecv, xsend, xrecv,
                   zsend_f, zrecv_f, keep_f, ysend_f, yrecv_f,
                   load_sem, send_sem, recv_sem):
     pipe, expert = lax.axis_index("pipe"), lax.axis_index("expert")
@@ -108,17 +109,13 @@
     blocks = nz * ny
     span = width * half_steps
     ring = range(1, nz)
-    z_pair = {}
-    for d in ring:
-        other_z = z
-        for k in range(nz.bit_length() - 1):
-            if d >> k & 1:
-                other_z = flip(other_z, 1 << k)
-        z_pair[d] = other_z
+    z_pair = {d: d - 1 + (d - 1 - z + nz) // nz for d in ring}
+    z_slot = {d: z - (z - z_pair[d] - 1 + nz) // nz for d in ring}
     core_peer = (x * CORES + 1 - c, expert)
     x_peer = ((1 - x) * CORES + c, expert)
     y_peer = (pipe, z * ny + 1 - y)
     z_peer = {d: (pipe, z_pair[d] * ny + y) for d in ring}
+    xz_peer = {d: ((1 - x) * CORES + c, z_pair[d] * ny + y) for d in ring}
 
     marks = {"load": {}, "recv": {}}
     sent_bytes = [0]
@@ -148,7 +145,7 @@
         return pl.multiple_of((where * CORES + part) * span + (s % half_steps) * width, 128)
 
     barrier = pltpu.get_barrier_semaphore()
-    peers = [core_peer, x_peer, y_peer] + [z_peer[d] for d in ring]
+    peers = [core_peer, x_peer, y_peer, *z_peer.values(), *xz_peer.values()]
     for peer in peers:
         pl.semaphore_signal(barrier, inc=1, device_id=peer, device_id_type=MESH_ID)
 
@@ -173,15 +170,17 @@
     with scope("barrier"):
         pl.semaphore_wait(barrier, len(peers))
 
-    for s in range(STEPS):
+    def own_out(s):
         loaded(("tok", s), tokv.at[s])
         own[s, z, y] = jnp.dot(
             select, tokv[s], preferred_element_type=jnp.float32).astype(jnp.bfloat16)
         for d in ring:
             send(("zin", s), own.at[s, z, y], own.at[s, z, y], z_peer[d])
         send(("yin", s), own.at[s, z, y], own.at[s, z, y], y_peer)
-        if s + 2 < STEPS:
-            load_weights(weight_order[s + 2])
+
+    own_out(0)
+    for s in weight_order[2:]:
+        load_weights(s)
     load(("dh",), dh.at[:, mine], dhv.at[c])
     send(("dhin",), dh.at[:, others], dhv.at[c], core_peer)
     lane = lax.broadcasted_iota(jnp.int32, (count, CORES * UNIT), 1).astype(jnp.float32)
@@ -234,9 +233,14 @@
                     acc[m] = term
             started.append(s)
 
+    own_out(1)
+    own_out(2)
     turn(0, 0)
+    own_out(3)
     turn(1, 0)
+    own_out(4)
     turn(0, 3)
+    own_out(5)
     turn(1, 3)
     relay(0)
     turn(1, 1)
@@ -323,7 +327,7 @@
             for d in ring:
                 for n in range(ny):
                     zsend_f[d - 1, n] = core_sum(s, (z_pair[d], n)).astype(jnp.bfloat16)
-                send(("zsum", s), zsend_f.at[d - 1], zrecv_f.at[d - 1], z_peer[d])
+                send(("zsum", s), zsend_f.at[d - 1], zrecv_f.at[z_slot[d]], z_peer[d])
             for n in range(ny):
                 keep_f[n] = core_sum(s, (z, n))
         else:
@@ -343,29 +347,35 @@
         ysend_f[...] = keep_f[1 - y].astype(jnp.bfloat16)
         send(("ysum", lead), ysend_f, yrecv_f, y_peer)
 
+    def y_sum(s, d):
+        landed(("ysum", s, d), yrecv.at[s, d])
+        return keep[s, d] + yrecv[s, d].astype(jnp.float32)
+
     def y_add(s):
         for d in ring:
-            landed(("ysum", s, d), yrecv.at[s, d])
-            zsend[s, d - 1] = (keep[s, d] + yrecv[s, d].astype(jnp.float32)).astype(jnp.bfloat16)
-            send(("zsum", s), zsend.at[s, d - 1], zrecv.at[s, d - 1], z_peer[d])
+            zsend[s, d - 1] = y_sum(s, d).astype(jnp.bfloat16)
+            send(("zsum", s), zsend.at[s, d - 1], zrecv.at[s, z_slot[d]],
+                 (xz_peer if s < half_steps else z_peer)[d])
+
+    def hand_over(s):
+        xsend[s] = y_sum(s, 0)
+        send(("xsum", s), xsend.at[s], xrecv.at[s], x_peer)
 
     def finish(s):
         if s == lead:
             landed(("ysum", s), yrecv_f)
             done = keep_f[y] + yrecv_f[...].astype(jnp.float32)
         else:
-            landed(("ysum", s, 0), yrecv.at[s, 0])
-            fin[s] = keep[s, 0] + yrecv[s, 0].astype(jnp.float32)
+            if s < half_steps:
+                landed(("xsum", s), xrecv.at[s])
+                done = xrecv[s]
+            else:
+                done = y_sum(s, 0)
             landed(("zsum", s), zrecv.at[s])
-            done = fin[s]
             for d in ring:
                 done = done + zrecv[s, d - 1].astype(jnp.float32)
         cols = slice((s % half_steps) * width, (s % half_steps + 1) * width)
-        if s < half_steps:
-            xsend[s] = done
-            send(("xsum",), xsend.at[s], slots.at[x, :, cols], x_peer)
-        else:
-            slots[x, :, cols] = done
+        slots[1 - x if s < half_steps else x, :, cols] = done
 
     back_other(0)
     back_own(0)
@@ -382,24 +392,26 @@
     back_other(4)
     core_add(2)
     y_add(0)
+    hand_over(0)
     back_own(4)
     back_other(5)
     core_add(4)
     back_own(5)
     y_add(1)
+    hand_over(1)
     core_add(5)
     y_add(2)
+    hand_over(2)
     lead_add()
     y_add(4)
+    y_add(5)
     finish(0)
-    y_add(5)
     finish(1)
     finish(2)
     finish(3)
     finish(4)
     finish(5)
 
-    landed(("xsum",), slots.at[0])
     loaded(("hid",), hst.at[0])
     landed(("hidin",), hst.at[0])
     with scope("sent"):
@@ -418,7 +430,7 @@
     half_steps = STEPS // 2
     bf, f32 = jnp.bfloat16, jnp.float32
     loads = STEPS * 2 + 2
-    recvs = STEPS * 5 + (STEPS - 1) * nz + 1 + STEPS + 3
+    recvs = STEPS * 5 + (STEPS - 1) * nz + 1 + STEPS + 5
     hbm = pl.BlockSpec(memory_space=pl.ANY)
     vmem = pl.BlockSpec(memory_space=pltpu.VMEM)
     flops = 8 * blocks * UNIT * features * half
@@ -451,7 +463,7 @@
             pltpu.VMEM((STEPS, nz, UNIT, width), bf),
             pltpu.VMEM((STEPS, nz - 1, UNIT, width), bf),
             pltpu.VMEM((STEPS, nz - 1, UNIT, width), bf),
-            pltpu.VMEM((STEPS, UNIT, width), f32),
+            pltpu.VMEM((half_steps, UNIT, width), f32),
             pltpu.VMEM((half_steps, UNIT, width), f32),
             pltpu.VMEM((nz - 1, ny, UNIT, width), bf),
             pltpu.VMEM((nz - 1, ny, UNIT, width), bf),

time: 40.7 us -> 39.8 us (0.978)
  Pallas kernels: 39.7 us -> 38.8 us
    pallas_call x1, Pallas kernels: 38.2 us -> 37.7 us  [fused_body(): pl.pallas_call(functools.partial(expert_kernel, nz, ny), out_shape=(pltpu...]
where the time goes in v3:
time: 39.8 us; the launch traced here: 39.6 us
  Pallas kernels  38.8 us (97%)
  between operations  0.8 us (2%)
    pallas_call x1, Pallas kernels, fused_body(): pl.pallas_call(functools.partial(expert_kernel, nz, ny), out_shape=(pltpu...  37.7 us
    pallas_call x1, Pallas kernels, fused_body(): pl.pallas_call(place_kernel, out_shape=(jax.ShapeDtypeStruct((count, half...  1.14 us

profile of v3, /device:TPU:0, one launch (start us, length us, event | category | flops | bytes accessed | tf_op | source)
XLA Modules:
  0.0 39.6 jit_solution(14252365485653253224)
XLA Ops:
  0.6 37.7 %shard_map.68 = (bf16[64,2048]{1,0:T(8,128)(2,1)S(1)}, f32[2,16,1536]{2,1,0:T(8,128)S(1)}, f32[128,32]{1,0:T(8,128)S(1)}) custom-call(bf16[128,6144]{1,0:T(8,128)(2,1)} %tok.1, s32[2,128]{1,0:T(2,128)} %bitcast.1, bf16[6144,2048]{1,0:T(8,128)(2,1)} %gate.1, bf16[6144,2048]{1,0:T(8,128)(2,1)} %up.1, bf16[64,2048]{1,0:T(8,128)(2,1)} %dh.1), custom_call_target="tpu_custom_call" | custom-call | flops 6442450944 | bytes 25165824 | tf_op jit(solution)/shard_map/pallas_call | solution.py:438
  38.3 1.1 %shard_map.69 = (f32[128,1536]{1,0:T(8,128)}, bf16[64,2048]{1,0:T(8,128)(2,1)}) custom-call(f32[128,32]{1,0:T(8,128)S(1)} %get-tuple-element.7.placed, f32[2,16,1536]{2,1,0:T(8,128)S(1)} %get-tuple-element.8.slots, bf16[64,2048]{1,0:T(8,128)(2,1)S(1)} %get-tuple-element.9.hid_in), custom_call_target="tpu_custom_call" | custom-call | tf_op jit(solution)/shard_map/pallas_call | solution.py:482

commit v4 on v3

--- a/solution.py
+++ b/solution.py
@@ -120,8 +120,13 @@
     marks = {"load": {}, "recv": {}}
     sent_bytes = [0]
 
+    def reuse(key):
+        if key[0] == "ysum" and key[2:] in ((), (1,)):
+            return ("zin", key[1])
+        return ("yin", key[1]) if key[0] == "csum" and not key[2] else key
+
     def mark(kind, key):
-        return marks[kind].setdefault(key, len(marks[kind]))
+        return marks[kind].setdefault(reuse(key), len(marks[kind]))
 
     def load(key, src, dst):
         pltpu.make_async_copy(src, dst, load_sem.at[mark("load", key)]).start()
@@ -137,7 +142,7 @@
 
     def landed(key, ref):
         with scope("_".join(str(k) for k in key)):
-            pltpu.make_async_copy(ref, ref, recv_sem.at[marks["recv"][key]]).wait()
+            pltpu.make_async_copy(ref, ref, recv_sem.at[marks["recv"][reuse(key)]]).wait()
 
     def offset(other, s):
         part = c if other == 0 else 1 - c
@@ -402,8 +407,8 @@
     core_add(5)
     y_add(2)
     hand_over(2)
+    y_add(4)
     lead_add()
-    y_add(4)
     y_add(5)
     finish(0)
     finish(1)
@@ -430,7 +435,7 @@
     half_steps = STEPS // 2
     bf, f32 = jnp.bfloat16, jnp.float32
     loads = STEPS * 2 + 2
-    recvs = STEPS * 5 + (STEPS - 1) * nz + 1 + STEPS + 5
+    recvs = STEPS * 5 + (STEPS - 1) * (nz - 1) + STEPS // 2 + 2
     hbm = pl.BlockSpec(memory_space=pl.ANY)
     vmem = pl.BlockSpec(memory_space=pltpu.VMEM)
     flops = 8 * blocks * UNIT * features * half

time: 39.8 us -> 39.6 us (level)
  no operation moved by 1% of the time
where the time goes in v4:
time: 39.6 us; the launch traced here: 39.5 us
  Pallas kernels  38.7 us (98%)
  between operations  0.8 us (2%)
    pallas_call x1, Pallas kernels, fused_body(): pl.pallas_call(functools.partial(expert_kernel, nz, ny), out_shape=(pltpu...  37.5 us
    pallas_call x1, Pallas kernels, fused_body(): pl.pallas_call(place_kernel, out_shape=(jax.ShapeDtypeStruct((count, half...  1.14 us

profile of v4, /device:TPU:0, one launch (start us, length us, event | category | flops | bytes accessed | tf_op | source)
XLA Modules:
  0.0 39.5 jit_solution(15171874396062137074)
XLA Ops:
  0.6 37.5 %shard_map.68 = (bf16[64,2048]{1,0:T(8,128)(2,1)S(1)}, f32[2,16,1536]{2,1,0:T(8,128)S(1)}, f32[128,32]{1,0:T(8,128)S(1)}) custom-call(bf16[128,6144]{1,0:T(8,128)(2,1)} %tok.1, s32[2,128]{1,0:T(2,128)} %bitcast.1, bf16[6144,2048]{1,0:T(8,128)(2,1)} %gate.1, bf16[6144,2048]{1,0:T(8,128)(2,1)} %up.1, bf16[64,2048]{1,0:T(8,128)(2,1)} %dh.1), custom_call_target="tpu_custom_call" | custom-call | flops 6442450944 | bytes 25165824 | tf_op jit(solution)/shard_map/pallas_call | solution.py:443
  38.2 1.1 %shard_map.69 = (f32[128,1536]{1,0:T(8,128)}, bf16[64,2048]{1,0:T(8,128)(2,1)}) custom-call(f32[128,32]{1,0:T(8,128)S(1)} %get-tuple-element.7.placed, f32[2,16,1536]{2,1,0:T(8,128)S(1)} %get-tuple-element.8.slots, bf16[64,2048]{1,0:T(8,128)(2,1)S(1)} %get-tuple-element.9.hid_in), custom_call_target="tpu_custom_call" | custom-call | tf_op jit(solution)/shard_map/pallas_call | solution.py:487
